TPU v7x, 32 devices: a whole 2x2x4 slice. The times are simulated.
32 devices in a mesh: cuts: 4 (over y, core), mesh: 8 (over z, x).
Axes of the slice: x: 2, y: 2, z: 4, core: 2. Of those that a mesh axis runs over, the one named last changes fastest.
Arguments:
- start_modes: float32 [128, 16384], P('cuts', 'mesh'), may hold values from -6 to 6
- connectivity: int32 [125, 256], P(None, 'mesh'), may hold values from 0 to 2047, as said below
- stiffness_weights: float32 [125, 256], P(None, 'mesh'), may hold values from 0.5 to 4
- shared_nodes: int32 [2, 4096], P(None, 'mesh'), may hold values from 0 to 2047, as said below
- node_mass: float32 [16384], P('mesh'), may hold values from 0.5 to 54
- centers: float32 [4], P('cuts'), may hold values from 20 to 200
- half_widths: float32 [4], P('cuts'), may hold values from 100 to 400
- keep_flags: int32 [4, 8], P('cuts'), may hold values 0 or 1
Outputs:
- filtered: float32 [128, 16384], P('cuts', 'mesh')
- edge_products: float32 [4, 8, 8], P('cuts')
- first_level: float32 [128, 16384], P('cuts', 'mesh')
Inputs may be any that keep to these rules, and one draw needn't show every extreme that they name: `connectivity`: within each partition: entry k = 25 a + 5 b + c names the element's GLL node (a, b, c); every node index of the partition is named by some element, and neighbouring elements name the same nodes on their common faces. `shared_nodes`: within each partition the 1024 entries are distinct; entry k of row 1 of partition p and entry k of row 0 of partition p + 1 are copies of the same node.
All inputs are finite; a program needn't handle non-finite values. No bound on the sum of `keep_flags` on one device may be relied on, other than what follows from the above.
Results may differ from a plain program's by a relative error of at most 0.0001.
Values sent between devices are 32-bit elements; how exact they have to be, the bound alone decides.
A program may use at most 64 MiB of HBM per device.

v0:
```python
import functools
import math

import jax
import jax.numpy as jnp
import numpy as np
from jax import lax
from jax.experimental import pallas as pl
from jax.experimental.pallas import tpu as pltpu
from jax.sharding import PartitionSpec as P

epsilon = 1e-06
LOW = 256
MESH = pl.DeviceIdType.MESH
bf16 = jnp.bfloat16
f32 = jnp.float32


def gll_derivative():
    points = np.array([-1.0, -math.sqrt(3.0 / 7.0), 0.0, math.sqrt(3.0 / 7.0), 1.0])
    barycentric = np.array(
        [1.0 / np.prod([points[j] - points[k] for k in range(5) if k != j]) for j in range(5)]
    )
    table = np.zeros((5, 5))
    for row_index in range(5):
        for col_index in range(5):
            if row_index != col_index:
                table[row_index, col_index] = (
                    barycentric[col_index]
                    / barycentric[row_index]
                    / (points[row_index] - points[col_index])
                )
        table[row_index, row_index] = -np.sum(table[row_index])
    return table


def apply5(table, u):
    even = [u[0] + u[4], u[1] + u[3]]
    odd = [u[0] - u[4], u[1] - u[3]]
    out = [None] * 5
    for i in range(2):
        s = [float((table[i, j] + table[i, 4 - j]) / 2) for j in range(2)]
        t = [float((table[i, j] - table[i, 4 - j]) / 2) for j in range(2)]
        p = s[0] * even[0] + s[1] * even[1] + float(table[i, 2]) * u[2]
        q = t[0] * odd[0] + t[1] * odd[1]
        out[i] = q + p
        out[4 - i] = q - p
    t = [float((table[2, j] - table[2, 4 - j]) / 2) for j in range(2)]
    out[2] = t[0] * odd[0] + t[1] * odd[1]
    return out


def transpose4(x):
    lane = lax.broadcasted_iota(jnp.int32, x[0].shape, 1)
    left = lane < 64
    even = (lane % 64) < 32
    y = [None] * 4
    for g in range(2):
        a, b = x[g], x[g + 2]
        y[g] = jnp.where(left, a, pltpu.roll(b, 64, 1))
        y[g + 2] = jnp.where(left, pltpu.roll(a, 64, 1), b)
    z = [None] * 4
    for g in (0, 2):
        a, b = y[g], y[g + 1]
        z[g] = jnp.where(even, a, pltpu.roll(b, 32, 1))
        z[g + 1] = jnp.where(even, pltpu.roll(a, 96, 1), b)
    return z


def split2(x):
    high = x.astype(bf16)
    low = (x - high.astype(f32)).astype(bf16)
    return high, low


def kernel(
    n_mesh,
    n_cuts,
    total_nodes,
    v_ref,
    conn_ref,
    w_ref,
    shared_ref,
    mass_ref,
    center_ref,
    half_ref,
    keep_ref,
    filt_ref,
    edge_ref,
    level_ref,
    conn_s,
    onehot,
    mask_f,
    mask_b,
    sh_onehot,
    sh_mask_f,
    sh_mask_b,
    w_s,
    u_s,
    r_s,
    src_s,
    scat_s,
    sh_scat_s,
    first_s,
    second_s,
    tx,
    rx,
    edge_tx,
    edge_rx,
    block,
    blocks,
    halo_send,
    halo_recv,
    edge_send,
    edge_recv,
    sum_send,
    sum_recv,
):
    me = lax.axis_index("mesh")
    cut = lax.axis_index("cuts")
    modes, nodes = v_ref.shape
    groups = modes // 8
    highs = nodes // LOW
    local, elements = conn_ref.shape
    shared = shared_ref.shape[1]
    edge_count = keep_ref.shape[1]
    table = gll_derivative()

    barrier = pltpu.get_barrier_semaphore()

    def greet(d, carry):
        pl.semaphore_signal(
            barrier,
            inc=1,
            device_id={"mesh": lax.rem(me + d, n_mesh)},
            device_id_type=MESH,
        )
        return carry

    lax.fori_loop(1, n_mesh, greet, 0)

    @pl.when(cut > 0)
    def _():
        pl.semaphore_signal(
            barrier, inc=1, device_id={"cuts": cut - 1}, device_id_type=MESH
        )

    @pl.when(cut < n_cuts - 1)
    def _():
        pl.semaphore_signal(
            barrier, inc=1, device_id={"cuts": cut + 1}, device_id_type=MESH
        )

    conn_s[...] = jnp.full(conn_s.shape, -1, jnp.int32)
    conn_s[0:local, :] = conn_ref[...]
    chunks = conn_s.shape[0] // 4
    index = jnp.concatenate(
        [conn_s[pl.ds(q, chunks, stride=4), :] for q in range(4)], axis=1
    )
    row_low = lax.broadcasted_iota(jnp.int32, (LOW, 128), 0)
    row_high = lax.broadcasted_iota(jnp.int32, (highs, 128), 0)

    def tables(row, cols, hot, mf, mb):
        low = row & (LOW - 1)
        high = row >> 8
        one = (row_low == low).astype(f32).astype(bf16)
        hot[0:LOW, cols] = one
        hot[LOW:, cols] = one
        m = (row_high == high).astype(f32)
        mf[:, cols] = m
        for h in range(highs):
            mb[h, :, cols] = jnp.broadcast_to(m[h : h + 1], (16, 128)).astype(bf16)

    for r in range(chunks):
        tables(index[r : r + 1], slice(r * 128, r * 128 + 128), onehot, mask_f, mask_b)
    per_row = shared // 128
    for r in range(2 * per_row):
        row = shared_ref[r // per_row : r // per_row + 1, r % per_row * 128 : r % per_row * 128 + 128]
        tables(row, slice(r * 128, r * 128 + 128), sh_onehot, sh_mask_f, sh_mask_b)
    w4 = jnp.concatenate([w_ref[...]] * 4, axis=1)
    for k in range(local):
        w_s[k] = jnp.broadcast_to(w4[k : k + 1], (8, 128))
    r_s[local:] = jnp.zeros((r_s.shape[0] - local, 8, 128), f32)

    inv_mass = 1.0 / mass_ref[...]
    center = center_ref[0]
    inv_half = 1.0 / jnp.full((1, 128), half_ref[0], f32)[:, 0:1]

    def load_source(x):
        high, low = split2(x)
        for h in range(highs):
            src_s[h * modes : (h + 1) * modes, 0:LOW] = high[:, h * LOW : (h + 1) * LOW]
            src_s[h * modes : (h + 1) * modes, LOW:] = low[:, h * LOW : (h + 1) * LOW]

    def gather(hot, mf, cols):
        res = jnp.dot(src_s[...], hot[:, cols], preferred_element_type=f32)
        out = res[0:modes] * mf[0:1, cols]
        for h in range(1, highs):
            out = out + res[h * modes : (h + 1) * modes] * mf[h : h + 1, cols]
        return out

    def place(x, dst, mb, cols):
        high, low = split2(x)
        both = jnp.concatenate([high, low], axis=0)
        for h in range(highs):
            m = mb[h, :, cols]
            for i in range(2 * modes // 16):
                dst[h * 2 * modes + i * 16 : h * 2 * modes + i * 16 + 16, cols] = (
                    both[i * 16 : i * 16 + 16] * m
                )

    def scatter(dst, hot):
        res = lax.dot_general(
            dst[...],
            hot[0:LOW, :],
            (((1,), (1,)), ((), ())),
            preferred_element_type=f32,
        )
        return jnp.concatenate(
            [
                res[h * 2 * modes : h * 2 * modes + modes]
                + res[h * 2 * modes + modes : (h + 1) * 2 * modes]
                for h in range(highs)
            ],
            axis=1,
        )

    def axis_pass(base_of, stride, first):
        def line(l, carry):
            base = base_of(l)
            u = [u_s[base + i * stride] for i in range(5)]
            g = apply5(table, u)
            g = [g[i] * w_s[base + i * stride] for i in range(5)]
            back = apply5(table.T, g)
            for i in range(5):
                k = base + i * stride
                r_s[k] = back[i] if first else r_s[k] + back[i]
            return carry

        lax.fori_loop(0, 25, line, 0, unroll=5)

    def halo(step):
        up = pltpu.make_async_remote_copy(
            src_ref=tx.at[step, 1],
            dst_ref=rx.at[step, 0],
            send_sem=halo_send.at[step, 0],
            recv_sem=halo_recv.at[step, 0],
            device_id={"mesh": lax.rem(me + 1, n_mesh)},
            device_id_type=MESH,
        )
        down = pltpu.make_async_remote_copy(
            src_ref=tx.at[step, 0],
            dst_ref=rx.at[step, 1],
            send_sem=halo_send.at[step, 1],
            recv_sem=halo_recv.at[step, 1],
            device_id={"mesh": lax.rem(me + n_mesh - 1, n_mesh)},
            device_id_type=MESH,
        )
        return up, down

    @pl.when(me == 0)
    def _():
        for step in range(2):
            rx[step, 0] = jnp.zeros((modes, shared), f32)

    @pl.when(me == n_mesh - 1)
    def _():
        for step in range(2):
            rx[step, 1] = jnp.zeros((modes, shared), f32)

    @pl.when(cut == 0)
    def _():
        edge_rx[...] = jnp.zeros(edge_rx.shape, f32)

    def operate(x, step):
        load_source(x)
        for t in range(chunks // 2):
            out = gather(onehot, mask_f, slice(t * 256, t * 256 + 256))
            for half in range(2):
                r = 2 * t + half
                piece = [
                    out[g * 8 : g * 8 + 8, half * 128 : half * 128 + 128] for g in range(4)
                ]
                for q, y in enumerate(transpose4(piece)):
                    u_s[4 * r + q] = y
        axis_pass(lambda l: 5 * l, 1, True)
        axis_pass(lambda l: 25 * (l // 5) + l % 5, 5, False)
        axis_pass(lambda l: l, 25, False)
        for r in range(chunks):
            piece = transpose4([r_s[4 * r + q] for q in range(4)])
            place(
                jnp.concatenate(piece, axis=0), scat_s, mask_b, slice(r * 128, r * 128 + 128)
            )
        applied = scatter(scat_s, onehot)
        load_source(applied)
        for t in range(2 * shared // 256):
            out = gather(sh_onehot, sh_mask_f, slice(t * 256, t * 256 + 256))
            at = t * 256
            tx[step, at // shared, :, at % shared : at % shared + 256] = out
        if step == 0:
            pl.semaphore_wait(
                barrier,
                n_mesh - 1 + jnp.minimum(cut, 1) + jnp.minimum(n_cuts - 1 - cut, 1),
            )
        up, down = halo(step)

        @pl.when(me < n_mesh - 1)
        def _():
            up.start()

        @pl.when(me > 0)
        def _():
            down.start()

        @pl.when(me > 0)
        def _():
            up.wait_recv()

        @pl.when(me < n_mesh - 1)
        def _():
            down.wait_recv()

        for side in range(2):
            for j in range(per_row):
                x_in = rx[step, side, :, j * 128 : j * 128 + 128]
                at = (side * per_row + j) * 128
                place(x_in, sh_scat_s, sh_mask_b, slice(at, at + 128))
        return (applied + scatter(sh_scat_s, sh_onehot)) * inv_mass

    start = v_ref[...]
    first_s[...] = (operate(start, 0) - center * start) * inv_half
    first = first_s[...]
    mass = mass_ref[...]
    first_sum = jnp.sum(mass * first * first, axis=1, keepdims=True)
    second_s[...] = 2.0 * (operate(first, 1) - center * first_s[...]) * inv_half - v_ref[...]

    edge_tx[:, 0:nodes] = second_s[modes - edge_count :, :]
    edge_tx[:, nodes:] = jnp.broadcast_to(first_sum[modes - edge_count :], (edge_count, 128))
    edge_copy = pltpu.make_async_remote_copy(
        src_ref=edge_tx,
        dst_ref=edge_rx,
        send_sem=edge_send,
        recv_sem=edge_recv,
        device_id={"cuts": lax.rem(cut + 1, n_cuts)},
        device_id_type=MESH,
    )

    @pl.when(cut < n_cuts - 1)
    def _():
        edge_copy.start()

    second = second_s[...]
    second_sum = jnp.sum(mass * second * second, axis=1, keepdims=True)

    def columns(a, b):
        lane = lax.broadcasted_iota(jnp.int32, (a.shape[0], 128), 1)
        return jnp.where(lane == 0, a, jnp.where(lane == 1, b, 0.0))

    block[0:modes, :] = columns(first_sum, second_sum)
    block[modes + edge_count :, :] = jnp.zeros((edge_count, 128), f32)

    @pl.when(cut > 0)
    def _():
        edge_copy.wait_recv()

    received = edge_rx[:, 0:nodes]
    weighted = received * mass
    block[modes : modes + edge_count, :] = columns(
        edge_rx[:, nodes:][:, 0:1], jnp.sum(weighted * received, axis=1, keepdims=True)
    )
    inner = lax.dot_general(
        weighted,
        second,
        (((1,), (1,)), ((), ())),
        preferred_element_type=f32,
        precision=lax.Precision.HIGHEST,
    )
    block[modes + edge_count :, 0:modes] = inner

    def sum_copy(d):
        return pltpu.make_async_remote_copy(
            src_ref=block,
            dst_ref=blocks.at[me],
            send_sem=sum_send.at[d],
            recv_sem=sum_recv.at[d],
            device_id={"mesh": lax.rem(me + d, n_mesh)},
            device_id_type=MESH,
        )

    def start_sum(d, carry):
        sum_copy(d).start()
        return carry

    lax.fori_loop(1, n_mesh, start_sum, 0)
    blocks[me] = block[...]

    def wait_sum(d, carry):
        sum_copy(d).wait_recv()
        return carry

    lax.fori_loop(1, n_mesh, wait_sum, 0)
    total = lax.fori_loop(1, n_mesh, lambda i, acc: acc + blocks[i], blocks[0])

    scale = lax.rsqrt(total[:, 0:1] / total_nodes + epsilon)
    own = scale * lax.rsqrt(scale * scale * total[:, 1:2] / total_nodes + epsilon)
    level_ref[...] = first_s[...] * scale[0:modes]
    filt_ref[...] = second_s[...] * own[0:modes]
    eye = lax.broadcasted_iota(jnp.int32, (modes, modes), 0) == lax.broadcasted_iota(
        jnp.int32, (modes, modes), 1
    )
    own_row = jnp.sum(
        jnp.where(eye, jnp.broadcast_to(own[0:modes], (modes, modes)), 0.0),
        axis=0,
        keepdims=True,
    )
    products = (
        total[modes + edge_count :, 0:edge_count]
        * own[modes : modes + edge_count]
        * own_row[:, 0:edge_count]
        * keep_ref[...].astype(f32)
        * (1.0 / math.sqrt(total_nodes))
    )
    edge_ref[...] = products

    for step in range(2):
        up, down = halo(step)

        @pl.when(me < n_mesh - 1)
        def _():
            up.wait_send()

        @pl.when(me > 0)
        def _():
            down.wait_send()

    @pl.when(cut < n_cuts - 1)
    def _():
        edge_copy.wait_send()

    def wait_sent(d, carry):
        sum_copy(d).wait_send()
        return carry

    lax.fori_loop(1, n_mesh, wait_sent, 0)


def per_device(
    start_modes,
    connectivity,
    stiffness_weights,
    shared_nodes,
    node_mass,
    centers,
    half_widths,
    keep_flags,
):
    n_mesh = lax.axis_size("mesh")
    n_cuts = lax.axis_size("cuts")
    modes, nodes = start_modes.shape
    local, elements = connectivity.shape
    shared = shared_nodes.shape[1]
    edge_count = keep_flags.shape[1]
    highs = nodes // LOW
    padded = -(-local // 8) * 8
    entries = padded * elements
    vmem = pl.BlockSpec(memory_space=pltpu.VMEM)
    smem = pl.BlockSpec(memory_space=pltpu.SMEM)
    dma = pltpu.SemaphoreType.DMA
    filtered, products, level = pl.pallas_call(
        functools.partial(kernel, n_mesh, n_cuts, nodes * n_mesh),
        out_shape=(
            jax.ShapeDtypeStruct((modes, nodes), f32),
            jax.ShapeDtypeStruct((edge_count, edge_count), f32),
            jax.ShapeDtypeStruct((modes, nodes), f32),
        ),
        in_specs=[vmem, vmem, vmem, vmem, vmem, smem, smem, vmem],
        out_specs=(vmem, vmem, vmem),
        scratch_shapes=[
            pltpu.VMEM((padded, elements), jnp.int32),
            pltpu.VMEM((2 * LOW, entries), bf16),
            pltpu.VMEM((highs, entries), f32),
            pltpu.VMEM((highs, 16, entries), bf16),
            pltpu.VMEM((2 * LOW, 2 * shared), bf16),
            pltpu.VMEM((highs, 2 * shared), f32),
            pltpu.VMEM((highs, 16, 2 * shared), bf16),
            pltpu.VMEM((padded, 8, 128), f32),
            pltpu.VMEM((padded, 8, 128), f32),
            pltpu.VMEM((padded, 8, 128), f32),
            pltpu.VMEM((highs * modes, 2 * LOW), bf16),
            pltpu.VMEM((highs * 2 * modes, entries), bf16),
            pltpu.VMEM((highs * 2 * modes, 2 * shared), bf16),
            pltpu.VMEM((modes, nodes), f32),
            pltpu.VMEM((modes, nodes), f32),
            pltpu.VMEM((2, 2, modes, shared), f32),
            pltpu.VMEM((2, 2, modes, shared), f32),
            pltpu.VMEM((edge_count, nodes + 128), f32),
            pltpu.VMEM((edge_count, nodes + 128), f32),
            pltpu.VMEM((modes + 2 * edge_count, 128), f32),
            pltpu.VMEM((n_mesh, modes + 2 * edge_count, 128), f32),
            dma((2, 2)),
            dma((2, 2)),
            dma,
            dma,
            dma((n_mesh,)),
            dma((n_mesh,)),
        ],
        compiler_params=pltpu.CompilerParams(collective_id=0, has_side_effects=True),
    )(
        start_modes,
        connectivity,
        stiffness_weights,
        shared_nodes,
        node_mass.reshape(1, nodes),
        centers,
        half_widths,
        keep_flags,
    )
    return filtered, products[None], level


def solution(mesh):
    return jax.shard_map(
        per_device,
        mesh=mesh,
        in_specs=(
            P("cuts", "mesh"),
            P(None, "mesh"),
            P(None, "mesh"),
            P(None, "mesh"),
            P("mesh"),
            P("cuts"),
            P("cuts"),
            P("cuts", None),
        ),
        out_specs=(P("cuts", "mesh"), P("cuts", None, None), P("cuts", "mesh")),
        check_vma=False,
    )
```

profile of v0, /device:TPU:0, one launch (start us, length us, event | category | flops | bytes accessed | tf_op | source)
XLA Modules:
  0.0 42.8 jit_solution(7441429807201288245)
XLA Ops:
  1.9 0.0 copy-start.1
  1.9 1.5 %copy.11.conn_ref = s32[125,32]{1,0:T(8,128)} copy(s32[125,32]{0,1:T(8,128)} %param.9) | data formatting | bytes 32000 | tf_op args[1]
  3.4 0.0 copy-done.1
  3.4 0.7 %copy.12.w_ref = f32[125,32]{1,0:T(8,128)} copy(f32[125,32]{0,1:T(8,128)S(1)} %copy-done.1) | data formatting | bytes 32000 | tf_op args[2]
  4.1 35.7 %shard_map.103 = (f32[32,2048]{1,0:T(8,128)}, f32[8,8]{1,0:T(8,128)}, f32[32,2048]{1,0:T(8,128)}) custom-call(f32[32,2048]{1,0:T(8,128)} %v_ref.1, s32[125,32]{1,0:T(8,128)} %copy.11.conn_ref, f32[125,32]{1,0:T(8,128)} %copy.12.w_ref, s32[2,512]{1,0:T(2,128)} %shared_ref.1, f32[1,2048]{1,0:T(1,128)} %bitcast.2, f32[1]{0:T(128)S(6)} %copy.16.center_ref, ...), custom_call_target="tpu_custom_call" | custom-call | tf_op jit(solution)/shard_map/pallas_call | solution.py:469
  39.8 0.0 copy-start.2
  39.8 0.0 copy-start
  39.8 1.7 %copy.18 = f32[32,2048]{1,0:T(8,128)} copy(f32[32,2048]{1,0:T(8,128)} %get-tuple-element.12) | data formatting | bytes 524288
  41.5 0.0 copy-done.2
  41.5 0.6 %copy.19 = f32[1,8,8]{2,1,0:T(8,128)} copy(f32[1,8,8]{2,1,0:T(8,128)S(1)} %bitcast.3) | data formatting | bytes 512
  42.1 0.0 copy-done
  42.1 0.7 %copy.20 = f32[32,2048]{1,0:T(8,128)} copy(f32[32,2048]{1,0:T(8,128)S(1)} %copy-done) | data formatting | bytes 524288
Async XLA Ops:
  1.9 1.5 %copy-start.1 = (f32[125,32]{0,1:T(8,128)S(1)}, f32[125,32]{0,1:T(8,128)}, u32[]{:S(2)}) copy-start(f32[125,32]{0,1:T(8,128)} %param.10) | copy-start | bytes 48004
  39.8 1.7 %copy-start.2 = (f32[8,8]{1,0:T(8,128)S(1)}, f32[8,8]{1,0:T(8,128)}, u32[]{:S(2)}) copy-start(f32[8,8]{1,0:T(8,128)} %get-tuple-element.7) | copy-start | bytes 772
  39.8 2.3 %copy-start = (f32[32,2048]{1,0:T(8,128)S(1)}, f32[32,2048]{1,0:T(8,128)}, u32[]{:S(2)}) copy-start(f32[32,2048]{1,0:T(8,128)} %get-tuple-element.14) | copy-start | bytes 786436
where the time goes:
time: 43.1 us; the launch traced here: 42.8 us
  Pallas kernels  35.7 us (83%)
  local copies, waits for them, and re-layouts  5.21 us (12%)
  between operations  1.96 us (5%)
    pallas_call x1, Pallas kernels, per_device(): pl.pallas_call(functools.partial(kernel, n_mesh, n_cuts, nodes * n_mesh),...  35.7 us
    unnamed x11, local copies, waits for them, and re-layouts  5.21 us

commit v1 on v0

--- a/solution.py
+++ b/solution.py
@@ -84,10 +84,10 @@
     mass_ref,
     center_ref,
     half_ref,
-    keep_ref,
-    filt_ref,
-    edge_ref,
-    level_ref,
+    first_s,
+    second_s,
+    total_ref,
+    turn_s,
     conn_s,
     onehot,
     mask_f,
@@ -101,8 +101,6 @@
     src_s,
     scat_s,
     sh_scat_s,
-    first_s,
-    second_s,
     tx,
     rx,
     edge_tx,
@@ -121,9 +119,9 @@
     modes, nodes = v_ref.shape
     groups = modes // 8
     highs = nodes // LOW
-    local, elements = conn_ref.shape
+    elements, local = conn_ref.shape
     shared = shared_ref.shape[1]
-    edge_count = keep_ref.shape[1]
+    edge_count = edge_tx.shape[0]
     table = gll_derivative()
 
     barrier = pltpu.get_barrier_semaphore()
@@ -151,8 +149,11 @@
             barrier, inc=1, device_id={"cuts": cut + 1}, device_id_type=MESH
         )
 
-    conn_s[...] = jnp.full(conn_s.shape, -1, jnp.int32)
-    conn_s[0:local, :] = conn_ref[...]
+    turn_s[...] = jnp.full(turn_s.shape, -1.0, f32)
+    turn_s[0:elements, 0:local] = conn_ref[...].astype(f32)
+    turn_s[elements : 2 * elements, 0:local] = w_ref[...]
+    turned = turn_s[...].T
+    conn_s[...] = turned[:, 0:elements].astype(jnp.int32)
     chunks = conn_s.shape[0] // 4
     index = jnp.concatenate(
         [conn_s[pl.ds(q, chunks, stride=4), :] for q in range(4)], axis=1
@@ -168,7 +169,7 @@
         hot[LOW:, cols] = one
         m = (row_high == high).astype(f32)
         mf[:, cols] = m
-        for h in range(highs):
+        for h in range(highs if mb is not None else 0):
             mb[h, :, cols] = jnp.broadcast_to(m[h : h + 1], (16, 128)).astype(bf16)
 
     for r in range(chunks):
@@ -176,8 +177,8 @@
     per_row = shared // 128
     for r in range(2 * per_row):
         row = shared_ref[r // per_row : r // per_row + 1, r % per_row * 128 : r % per_row * 128 + 128]
-        tables(row, slice(r * 128, r * 128 + 128), sh_onehot, sh_mask_f, sh_mask_b)
-    w4 = jnp.concatenate([w_ref[...]] * 4, axis=1)
+        tables(row, slice(r * 128, r * 128 + 128), sh_onehot, sh_mask_f, None)
+    w4 = jnp.concatenate([turned[:, elements : 2 * elements]] * 4, axis=1)
     for k in range(local):
         w_s[k] = jnp.broadcast_to(w4[k : k + 1], (8, 128))
     r_s[local:] = jnp.zeros((r_s.shape[0] - local, 8, 128), f32)
@@ -272,7 +273,7 @@
     def _():
         edge_rx[...] = jnp.zeros(edge_rx.shape, f32)
 
-    def operate(x, step):
+    def operate(x, step, between):
         load_source(x)
         for t in range(chunks // 2):
             out = gather(onehot, mask_f, slice(t * 256, t * 256 + 256))
@@ -293,24 +294,27 @@
             )
         applied = scatter(scat_s, onehot)
         load_source(applied)
+        up, down = halo(step)
         for t in range(2 * shared // 256):
             out = gather(sh_onehot, sh_mask_f, slice(t * 256, t * 256 + 256))
             at = t * 256
             tx[step, at // shared, :, at % shared : at % shared + 256] = out
-        if step == 0:
-            pl.semaphore_wait(
-                barrier,
-                n_mesh - 1 + jnp.minimum(cut, 1) + jnp.minimum(n_cuts - 1 - cut, 1),
-            )
-        up, down = halo(step)
+            if at + 256 == shared:
+                if step == 0:
+                    pl.semaphore_wait(
+                        barrier,
+                        n_mesh - 1 + jnp.minimum(cut, 1) + jnp.minimum(n_cuts - 1 - cut, 1),
+                    )
+
+                @pl.when(me > 0)
+                def _():
+                    down.start()
 
         @pl.when(me < n_mesh - 1)
         def _():
             up.start()
 
-        @pl.when(me > 0)
-        def _():
-            down.start()
+        between()
 
         @pl.when(me > 0)
         def _():
@@ -328,12 +332,29 @@
         return (applied + scatter(sh_scat_s, sh_onehot)) * inv_mass
 
     start = v_ref[...]
-    first_s[...] = (operate(start, 0) - center * start) * inv_half
+    mass = mass_ref[...]
+    turn_s[...] = jnp.zeros(turn_s.shape, f32)
+
+    def masks():
+        for r in range(2 * per_row):
+            cols = slice(r * 128, r * 128 + 128)
+            for h in range(highs):
+                sh_mask_b[h, :, cols] = jnp.broadcast_to(
+                    sh_mask_f[h : h + 1, cols], (16, 128)
+                ).astype(bf16)
+
+    def first_column():
+        level = first_s[...]
+        lane = lax.broadcasted_iota(jnp.int32, (modes, 128), 1)
+        turn_s[0:modes, :] = jnp.where(
+            lane == 0, jnp.sum(mass * level * level, axis=1, keepdims=True), 0.0
+        )
+
+    first_s[...] = (operate(start, 0, masks) - center * start) * inv_half
     first = first_s[...]
-    mass = mass_ref[...]
-    first_sum = jnp.sum(mass * first * first, axis=1, keepdims=True)
-    second_s[...] = 2.0 * (operate(first, 1) - center * first_s[...]) * inv_half - v_ref[...]
-
+    second_s[...] = 2.0 * (operate(first, 1, first_column) - center * first_s[...]) * inv_half - v_ref[...]
+
+    first_sum = turn_s[0:modes, 0:1]
     edge_tx[:, 0:nodes] = second_s[modes - edge_count :, :]
     edge_tx[:, nodes:] = jnp.broadcast_to(first_sum[modes - edge_count :], (edge_count, 128))
     edge_copy = pltpu.make_async_remote_copy(
@@ -356,8 +377,7 @@
         lane = lax.broadcasted_iota(jnp.int32, (a.shape[0], 128), 1)
         return jnp.where(lane == 0, a, jnp.where(lane == 1, b, 0.0))
 
-    block[0:modes, :] = columns(first_sum, second_sum)
-    block[modes + edge_count :, :] = jnp.zeros((edge_count, 128), f32)
+    turn_s[0:modes, :] = columns(first_sum, second_sum)
 
     @pl.when(cut > 0)
     def _():
@@ -365,7 +385,7 @@
 
     received = edge_rx[:, 0:nodes]
     weighted = received * mass
-    block[modes : modes + edge_count, :] = columns(
+    turn_s[modes : modes + edge_count, :] = columns(
         edge_rx[:, nodes:][:, 0:1], jnp.sum(weighted * received, axis=1, keepdims=True)
     )
     inner = lax.dot_general(
@@ -375,7 +395,8 @@
         preferred_element_type=f32,
         precision=lax.Precision.HIGHEST,
     )
-    block[modes + edge_count :, 0:modes] = inner
+    turn_s[modes + edge_count : modes + 2 * edge_count, 0:modes] = inner
+    block[...] = turn_s[...].T[0:8]
 
     def sum_copy(d):
         return pltpu.make_async_remote_copy(
@@ -401,10 +422,38 @@
     lax.fori_loop(1, n_mesh, wait_sum, 0)
     total = lax.fori_loop(1, n_mesh, lambda i, acc: acc + blocks[i], blocks[0])
 
+    total_ref[...] = total
+
+    for step in range(2):
+        up, down = halo(step)
+
+        @pl.when(me < n_mesh - 1)
+        def _():
+            up.wait_send()
+
+        @pl.when(me > 0)
+        def _():
+            down.wait_send()
+
+    @pl.when(cut < n_cuts - 1)
+    def _():
+        edge_copy.wait_send()
+
+    def wait_sent(d, carry):
+        sum_copy(d).wait_send()
+        return carry
+
+    lax.fori_loop(1, n_mesh, wait_sent, 0)
+
+
+def finish(total_nodes, first_ref, second_ref, total_ref, keep_ref, filt_ref, edge_ref, level_ref):
+    modes = first_ref.shape[0]
+    edge_count = keep_ref.shape[1]
+    total = jnp.concatenate([total_ref[...], jnp.zeros((120, 128), f32)], axis=0).T
     scale = lax.rsqrt(total[:, 0:1] / total_nodes + epsilon)
     own = scale * lax.rsqrt(scale * scale * total[:, 1:2] / total_nodes + epsilon)
-    level_ref[...] = first_s[...] * scale[0:modes]
-    filt_ref[...] = second_s[...] * own[0:modes]
+    level_ref[...] = first_ref[...] * scale[0:modes]
+    filt_ref[...] = second_ref[...] * own[0:modes]
     eye = lax.broadcasted_iota(jnp.int32, (modes, modes), 0) == lax.broadcasted_iota(
         jnp.int32, (modes, modes), 1
     )
@@ -414,34 +463,13 @@
         keepdims=True,
     )
     products = (
-        total[modes + edge_count :, 0:edge_count]
+        total[modes + edge_count : modes + 2 * edge_count, 0:edge_count]
         * own[modes : modes + edge_count]
         * own_row[:, 0:edge_count]
         * keep_ref[...].astype(f32)
         * (1.0 / math.sqrt(total_nodes))
     )
-    edge_ref[...] = products
-
-    for step in range(2):
-        up, down = halo(step)
-
-        @pl.when(me < n_mesh - 1)
-        def _():
-            up.wait_send()
-
-        @pl.when(me > 0)
-        def _():
-            down.wait_send()
-
-    @pl.when(cut < n_cuts - 1)
-    def _():
-        edge_copy.wait_send()
-
-    def wait_sent(d, carry):
-        sum_copy(d).wait_send()
-        return carry
-
-    lax.fori_loop(1, n_mesh, wait_sent, 0)
+    edge_ref[0] = products
 
 
 def per_device(
@@ -466,16 +494,17 @@
     vmem = pl.BlockSpec(memory_space=pltpu.VMEM)
     smem = pl.BlockSpec(memory_space=pltpu.SMEM)
     dma = pltpu.SemaphoreType.DMA
-    filtered, products, level = pl.pallas_call(
+    first, second, total = pl.pallas_call(
         functools.partial(kernel, n_mesh, n_cuts, nodes * n_mesh),
         out_shape=(
             jax.ShapeDtypeStruct((modes, nodes), f32),
-            jax.ShapeDtypeStruct((edge_count, edge_count), f32),
             jax.ShapeDtypeStruct((modes, nodes), f32),
+            jax.ShapeDtypeStruct((8, 128), f32),
         ),
-        in_specs=[vmem, vmem, vmem, vmem, vmem, smem, smem, vmem],
+        in_specs=[vmem, vmem, vmem, vmem, vmem, smem, smem],
         out_specs=(vmem, vmem, vmem),
         scratch_shapes=[
+            pltpu.VMEM((128, 128), f32),
             pltpu.VMEM((padded, elements), jnp.int32),
             pltpu.VMEM((2 * LOW, entries), bf16),
             pltpu.VMEM((highs, entries), f32),
@@ -489,14 +518,12 @@
             pltpu.VMEM((highs * modes, 2 * LOW), bf16),
             pltpu.VMEM((highs * 2 * modes, entries), bf16),
             pltpu.VMEM((highs * 2 * modes, 2 * shared), bf16),
-            pltpu.VMEM((modes, nodes), f32),
-            pltpu.VMEM((modes, nodes), f32),
             pltpu.VMEM((2, 2, modes, shared), f32),
             pltpu.VMEM((2, 2, modes, shared), f32),
             pltpu.VMEM((edge_count, nodes + 128), f32),
             pltpu.VMEM((edge_count, nodes + 128), f32),
-            pltpu.VMEM((modes + 2 * edge_count, 128), f32),
-            pltpu.VMEM((n_mesh, modes + 2 * edge_count, 128), f32),
+            pltpu.VMEM((8, 128), f32),
+            pltpu.VMEM((n_mesh, 8, 128), f32),
             dma((2, 2)),
             dma((2, 2)),
             dma,
@@ -507,15 +534,23 @@
         compiler_params=pltpu.CompilerParams(collective_id=0, has_side_effects=True),
     )(
         start_modes,
-        connectivity,
-        stiffness_weights,
+        connectivity.T,
+        stiffness_weights.T,
         shared_nodes,
         node_mass.reshape(1, nodes),
         centers,
         half_widths,
-        keep_flags,
-    )
-    return filtered, products[None], level
+    )
+    return pl.pallas_call(
+        functools.partial(finish, nodes * n_mesh),
+        out_shape=(
+            jax.ShapeDtypeStruct((modes, nodes), f32),
+            jax.ShapeDtypeStruct((1, edge_count, edge_count), f32),
+            jax.ShapeDtypeStruct((modes, nodes), f32),
+        ),
+        in_specs=[vmem, vmem, vmem, vmem],
+        out_specs=(vmem, vmem, vmem),
+    )(first, second, total, keep_flags)
 
 
 def solution(mesh):

time: 43.1 us -> 37.3 us (0.87)
  local copies, waits for them, and re-layouts: 5.21 us -> 0 us
  Pallas kernels: 35.7 us -> 35.2 us
    unnamed x11 -> x0, local copies, waits for them, and re-layouts: 5.21 us -> none
    pallas_call x1, Pallas kernels: 35.7 us -> 33.2 us  [per_device(): pl.pallas_call(functools.partial(kernel, n_mesh, n_cuts, nodes * n_mesh),...]
    pallas_call x0 -> x1, Pallas kernels: none -> 2.06 us  [per_device(): pl.pallas_call(functools.partial(finish, nodes * n_mesh), out_shape=(jax....]
where the time goes in v1:
time: 37.3 us; the launch traced here: 37.2 us
  Pallas kernels  35.2 us (94%)
  between operations  1.93 us (5%)
    pallas_call x1, Pallas kernels, per_device(): pl.pallas_call(functools.partial(kernel, n_mesh, n_cuts, nodes * n_mesh),...  33.2 us
    pallas_call x1, Pallas kernels, per_device(): pl.pallas_call(functools.partial(finish, nodes * n_mesh), out_shape=(jax....  2.06 us

profile of v1, /device:TPU:0, one launch (start us, length us, event | category | flops | bytes accessed | tf_op | source)
XLA Modules:
  0.0 37.2 jit_solution(8842365025576962796)
XLA Ops:
  1.9 33.2 %shard_map.103 = (f32[32,2048]{1,0:T(8,128)}, f32[32,2048]{1,0:T(8,128)}, f32[8,128]{1,0:T(8,128)}) custom-call(f32[32,2048]{1,0:T(8,128)} %v_ref.1, s32[32,125]{1,0:T(8,128)} %bitcast.3, f32[32,125]{1,0:T(8,128)} %bitcast.4, s32[2,512]{1,0:T(2,128)} %shared_ref.1, f32[1,2048]{1,0:T(1,128)} %bitcast.5, f32[1]{0:T(128)S(6)} %copy.11.center_ref, ...), custom_call_target="tpu_custom_call" | custom-call | tf_op jit(solution)/shard_map/pallas_call | solution.py:497
  35.1 2.1 %shard_map.104 = (f32[32,2048]{1,0:T(8,128)}, f32[1,8,8]{2,1,0:T(8,128)}, f32[32,2048]{1,0:T(8,128)}) custom-call(f32[32,2048]{1,0:T(8,128)} %get-tuple-element.6.first_ref, f32[32,2048]{1,0:T(8,128)} %get-tuple-element.7.second_ref, f32[8,128]{1,0:T(8,128)} %get-tuple-element.8.total_ref, s32[1,8]{1,0:T(1,128)} %keep_ref.1), custom_call_target="tpu_custom_call" | custom-call | tf_op jit(solution)/shard_map/pallas_call | solution.py:544

commit v2 on v1

--- a/solution.py
+++ b/solution.py
@@ -184,8 +184,8 @@
     r_s[local:] = jnp.zeros((r_s.shape[0] - local, 8, 128), f32)
 
     inv_mass = 1.0 / mass_ref[...]
-    center = center_ref[0]
-    inv_half = 1.0 / jnp.full((1, 128), half_ref[0], f32)[:, 0:1]
+    center = center_ref[...]
+    inv_half = 1.0 / half_ref[...]
 
     def load_source(x):
         high, low = split2(x)
@@ -492,7 +492,6 @@
     padded = -(-local // 8) * 8
     entries = padded * elements
     vmem = pl.BlockSpec(memory_space=pltpu.VMEM)
-    smem = pl.BlockSpec(memory_space=pltpu.SMEM)
     dma = pltpu.SemaphoreType.DMA
     first, second, total = pl.pallas_call(
         functools.partial(kernel, n_mesh, n_cuts, nodes * n_mesh),
@@ -501,7 +500,7 @@
             jax.ShapeDtypeStruct((modes, nodes), f32),
             jax.ShapeDtypeStruct((8, 128), f32),
         ),
-        in_specs=[vmem, vmem, vmem, vmem, vmem, smem, smem],
+        in_specs=[vmem, vmem, vmem, vmem, vmem, vmem, vmem],
         out_specs=(vmem, vmem, vmem),
         scratch_shapes=[
             pltpu.VMEM((128, 128), f32),
@@ -538,8 +537,8 @@
         stiffness_weights.T,
         shared_nodes,
         node_mass.reshape(1, nodes),
-        centers,
-        half_widths,
+        centers.reshape(1, 1),
+        half_widths.reshape(1, 1),
     )
     return pl.pallas_call(
         functools.partial(finish, nodes * n_mesh),

time: 37.3 us -> 37.4 us (level)
  no operation moved by 1% of the time
where the time goes in v2:
time: 37.4 us; the launch traced here: 37.2 us
  Pallas kernels  35.2 us (94%)
  between operations  1.93 us (5%)
    pallas_call x1, Pallas kernels, per_device(): pl.pallas_call(functools.partial(kernel, n_mesh, n_cuts, nodes * n_mesh),...  33.2 us
    pallas_call x1, Pallas kernels, per_device(): pl.pallas_call(functools.partial(finish, nodes * n_mesh), out_shape=(jax....  2.06 us

profile of v2, /device:TPU:0, one launch (start us, length us, event | category | flops | bytes accessed | tf_op | source)
XLA Modules:
  0.0 37.2 jit_solution(13884910245594453172)
XLA Ops:
  1.9 33.2 %shard_map.103 = (f32[32,2048]{1,0:T(8,128)}, f32[32,2048]{1,0:T(8,128)}, f32[8,128]{1,0:T(8,128)}) custom-call(f32[32,2048]{1,0:T(8,128)} %v_ref.1, s32[32,125]{1,0:T(8,128)} %bitcast.7, f32[32,125]{1,0:T(8,128)} %bitcast.8, s32[2,512]{1,0:T(2,128)} %shared_ref.1, f32[1,2048]{1,0:T(1,128)} %bitcast.9, f32[1,1]{1,0:T(1,128)} %bitcast.5.center_ref, ...), custom_call_target="tpu_custom_call" | custom-call | tf_op jit(solution)/shard_map/pallas_call | solution.py:496
  35.1 2.1 %shard_map.104 = (f32[32,2048]{1,0:T(8,128)}, f32[1,8,8]{2,1,0:T(8,128)}, f32[32,2048]{1,0:T(8,128)}) custom-call(f32[32,2048]{1,0:T(8,128)} %get-tuple-element.6.first_ref, f32[32,2048]{1,0:T(8,128)} %get-tuple-element.7.second_ref, f32[8,128]{1,0:T(8,128)} %get-tuple-element.8.total_ref, s32[1,8]{1,0:T(1,128)} %keep_ref.1), custom_call_target="tpu_custom_call" | custom-call | tf_op jit(solution)/shard_map/pallas_call | solution.py:543
